TPU v7x, 32 devices: a whole 2x2x4 slice. The times are simulated.
32 devices in a mesh: seq: 8 (over z, y), head: 4 (over x, core).
Axes of the slice: x: 2, y: 2, z: 4, core: 2. Of those that a mesh axis runs over, the one named last changes fastest.
Arguments:
- queries: bfloat16 [4096, 2048], P('seq', 'head'), may hold values from -6 to 6
- keys: bfloat16 [4096, 2048], P('seq', 'head'), may hold values from -6 to 6
- values: bfloat16 [4096, 2048], P('seq', 'head'), may hold values from -6 to 6
- level_weights: int32 [16, 20], P('head'), may hold values from 1 to 8
- out_grad: bfloat16 [4096, 2048], P('seq'), may hold values from -6 to 6
Outputs:
- normed: bfloat16 [4096, 2048], P('seq', 'head')
- proj_grad: float32 [2048, 2048], P('seq', 'head')
All inputs are finite; a program needn't handle non-finite values.
Results may differ from a plain program's by a relative error of at most 0.0031.
Values sent between devices are 32-bit elements; how exact they have to be, the bound alone decides.
A program may use at most 64 MiB of HBM per device.

v0:
```python
import functools

import jax
import jax.numpy as jnp
from jax import lax
from jax.experimental import pallas as pl
from jax.experimental.pallas import tpu as pltpu
from jax.sharding import PartitionSpec as P

D = 2048
HEADS = 16
GROUP = 512
PIECES = 2
MESH = pl.DeviceIdType.MESH
NT = (((1,), (1,)), ((), ()))
TN = (((0,), (0,)), ((), ()))


def flip(index, mask):
    bit = 1
    while bit <= mask:
        if mask & bit:
            index = index + bit - 2 * bit * ((index // bit) % 2)
        bit *= 2
    return index


def matmul(a, b, dims=(((1,), (0,)), ((), ()))):
    return lax.dot_general(a, b, dims, preferred_element_type=jnp.float32)


def split(x):
    high = x.astype(jnp.bfloat16)
    return high, (x - high.astype(jnp.float32)).astype(jnp.bfloat16)


def kernel(
    line,
    heads,
    q_in,
    k_in,
    v_in,
    level_ref,
    grad_in,
    normed_ref,
    out_ref,
    q_ref,
    k_ref,
    v_ref,
    grad_ref,
    loads,
    state,
    pair_state,
    block,
    line_state,
    give,
    mix,
    turned,
    quarter,
    theirs,
    theirs_half,
    raw,
    came,
    squares,
    squares_in,
    root,
    root_in,
    part,
    rising,
    falling,
    state_send,
    state_recv,
    grad_send,
    grad_recv,
    square_send,
    square_recv,
    root_send,
    root_recv,
    pair_send,
    pair_recv,
    up_send,
    up_recv,
    down_send,
    down_recv,
):
    me = lax.axis_index("seq")
    head = lax.axis_index("head")
    place = me // 2
    side = me % 2
    other = flip(me, 1)
    above = me + 2
    below = me - 2
    tokens, width = q_ref.shape
    lanes = D // HEADS
    chunks = width // lanes
    half = chunks // 2
    rows = out_ref.shape[0]
    line_bits = line.bit_length() - 1
    head_bits = heads.bit_length() - 1
    share = line // heads
    piece = rows // PIECES
    stages = list(reversed(range(head_bits)))
    held = [[0]]
    for bit in stages:
        held.append(held[-1] + [r ^ (1 << bit) for r in held[-1]])
    scale = lanes ** (-0.5)
    low_end = place == 0
    high_end = place == line - 1

    def span(k):
        return slice(k * lanes, (k + 1) * lanes)

    pairs = ((k_in, k_ref), (v_in, v_ref), (grad_in, grad_ref), (q_in, q_ref))
    copies = [pltpu.make_async_copy(a, b, loads.at[i]) for i, (a, b) in enumerate(pairs)]
    for copy in copies:
        copy.start()

    barrier = pltpu.get_barrier_semaphore()

    def greet(device):
        pl.semaphore_signal(barrier, inc=1, device_id=device, device_id_type=MESH)

    greet({"seq": other})
    for b in range(line_bits):
        greet({"seq": flip(me, 2 << b)})
    for r in range(1, heads):
        greet({"head": flip(head, r)})

    @pl.when(place < line - 1)
    def _():
        greet({"seq": above})

    @pl.when(place > 0)
    def _():
        greet({"seq": below})

    def remote(src, dst, send, recv, device):
        return pltpu.make_async_remote_copy(
            src_ref=src,
            dst_ref=dst,
            send_sem=send,
            recv_sem=recv,
            device_id=device,
            device_id_type=MESH,
        )

    def state_copy():
        return remote(
            state.at[pl.ds((1 - side) * half, half)],
            pair_state,
            state_send.at[0],
            state_recv.at[0],
            {"seq": other},
        )

    def line_copy(b):
        return remote(
            block.at[b],
            line_state.at[b],
            state_send.at[1 + b],
            state_recv.at[1 + b],
            {"seq": flip(me, 2 << b)},
        )

    def give_copy():
        return remote(
            give,
            mix.at[pl.ds(side * half, half)],
            state_send.at[1 + line_bits],
            state_recv.at[1 + line_bits],
            {"seq": other},
        )

    def grad_copy(p):
        return remote(
            quarter.at[:, pl.ds(p * piece, piece)],
            theirs.at[pl.ds(head * share, share), pl.ds(p * piece, piece)],
            grad_send.at[0, p],
            grad_recv.at[0, p],
            {"seq": other},
        )

    def share_copy(r, bit, p):
        owned = theirs.at[pl.ds(flip(head, r) * share, share), pl.ds(p * piece, piece)]
        slot = r ^ (1 << bit)
        return remote(
            owned,
            owned,
            grad_send.at[slot, p],
            grad_recv.at[slot, p],
            {"head": flip(head, 1 << bit)},
        )

    def square_copy(r):
        return remote(
            squares,
            squares_in.at[r - 1],
            square_send.at[r - 1],
            square_recv.at[r - 1],
            {"head": flip(head, r)},
        )

    def root_copy():
        return remote(root, root_in, root_send.at[0], root_recv.at[0], {"seq": other})

    def pair_copy(k):
        return remote(raw.at[k], came.at[k], pair_send.at[k], pair_recv.at[k], {"seq": other})

    def up_copy(k, d):
        return remote(
            part.at[k, d], rising.at[k, d], up_send.at[k, d], up_recv.at[k, d], {"seq": above}
        )

    def down_copy(k, d):
        return remote(
            part.at[k, d], falling.at[k, d], down_send.at[k, d], down_recv.at[k, d], {"seq": below}
        )

    copies[0].wait()
    copies[1].wait()
    for h in range(chunks):
        state[h] = matmul(k_ref[:, span(h)], v_ref[:, span(h)], TN)
    peers = line_bits + heads + jnp.where(place > 0, 1, 0) + jnp.where(place < line - 1, 1, 0)
    pl.semaphore_wait(barrier, peers)
    state_copy().start()

    copies[2].wait()
    tile = max(rows, lanes)
    for j in range(grad_ref.shape[1] // tile):
        flat = grad_ref[:, j * tile : (j + 1) * tile].T
        for i in range(tile // rows):
            owner = j * (tile // rows) + i
            turned[owner % 2, owner // 2] = flat[i * rows : (i + 1) * rows]
    quarter[...] = turned[1 - side, pl.ds(head * share, share)].astype(jnp.float32)
    for p in range(PIECES):
        grad_copy(p).start()

    def forward(i, p):
        for r in held[i]:
            share_copy(r, stages[i], p).start()

    def collect(i, p):
        for r in held[i]:
            share_copy(r, stages[i], p).wait_recv()

    def near(h):
        weight = scale * level_ref[h, 0].astype(jnp.float32)
        scores = matmul(q_ref[:, span(h)], k_ref[:, span(h)], NT) * weight
        row = lax.broadcasted_iota(jnp.int32, scores.shape, 0)
        column = lax.broadcasted_iota(jnp.int32, scores.shape, 1)
        probs = jnp.where(column <= row, scores, 0.0).astype(jnp.bfloat16)
        raw[h] = matmul(probs, v_ref[:, span(h)])

    def level(i, number):
        return level_ref[side * half + i, number].astype(jnp.float32)

    copies[3].wait()
    own = pl.ds(side * half, half)
    state_copy().wait_recv()
    block[0] = state[own] + pair_state[...]
    done = 0
    for b in range(line_bits):
        upper = (place // (1 << b)) % 2
        last = b == line_bits - 1
        if last:

            @pl.when(upper == 0)
            def _():
                line_copy(b).start()
        else:
            line_copy(b).start()
        until = chunks * (b + 1) // line_bits
        for h in range(done, until):
            near(h)
        done = until
        if last:
            grad_copy(0).wait_recv()
            forward(0, 0)

            @pl.when(upper == 1)
            def _():
                line_copy(b).wait_recv()

            @pl.when(upper == 0)
            def _():
                line_state[b] = jnp.zeros(line_state.shape[1:], jnp.float32)
        else:
            line_copy(b).wait_recv()
            block[b + 1] = block[b] + line_state[b]
    for i in range(half):
        far = jnp.zeros((lanes, lanes), jnp.float32)
        for b in range(line_bits):
            upper = ((place // (1 << b)) % 2).astype(jnp.float32)
            far = far + (level(i, 2 + b) * upper) * line_state[b, i]
        first = level(i, 1)
        right = side.astype(jnp.float32)
        mix[side * half + i] = far + (first * right) * pair_state[i]
        give[i] = far + (first * (1.0 - right)) * state[side * half + i]
    give_copy().start()

    for p in range(1, PIECES):
        grad_copy(p).wait_recv()
        forward(0, p)
    give_copy().wait_recv()

    total = jnp.zeros((tokens, lanes), jnp.float32)
    for h in range(chunks):
        high, low = split(mix[h])
        query = q_ref[:, span(h)]
        value = raw[h] + scale * (matmul(query, high) + matmul(query, low))
        raw[h] = value
        if h == 0:
            pair_copy(0).start()
        total = total + value * value
    ones = jnp.ones((8, lanes), jnp.bfloat16)
    high, low = split(total)
    squares[...] = matmul(ones, high, NT) + matmul(ones, low, NT)
    for r in range(1, heads):
        square_copy(r).start()
    collect(0, 0)
    forward(1, 0)
    for r in range(1, heads):
        square_copy(r).wait_recv()
    whole = squares[...]
    for r in range(1, heads):
        whole = whole + squares_in[r - 1]
    root[...] = lax.rsqrt(whole / D + 1e-06)
    root_copy().start()
    for p in range(1, PIECES):
        collect(0, p)
        forward(1, p)
    inverse = root[...].T[:, :1]
    for h in range(chunks):
        normed_ref[:, span(h)] = (raw[h] * inverse).astype(jnp.bfloat16)
    pair_copy(0).wait_send()
    pair_copy(1).start()
    root_copy().wait_recv()
    their_inverse = root_in[...].T[:, :1]
    for i in range(1, head_bits):
        for p in range(PIECES):
            if i > 1:
                forward(i, p)
            collect(i, p)
    theirs_half[...] = theirs[...].reshape(theirs_half.shape).astype(jnp.bfloat16)

    def ends(k):
        @pl.when(low_end)
        def _():
            @pl.loop(0, line - 1)
            def _(i):
                up_copy(k, line - 1 - i).start()

        @pl.when(high_end)
        def _():
            @pl.loop(0, line - 1)
            def _(d):
                down_copy(k, d).start()

    def rise(k):
        @pl.loop(0, line - 1 - place)
        def _(i):
            d = line - 1 - i
            up_copy(k, d).wait_recv()
            part[k, d] = part[k, d] + rising[k, d]
            up_copy(k, d).start()

    def fall(k):
        @pl.loop(0, place)
        def _(d):
            down_copy(k, d).wait_recv()
            part[k, d] = part[k, d] + falling[k, d]
            down_copy(k, d).start()

    def middle(k):
        @pl.when(jnp.logical_and(place > 0, place < line // 2))
        def _():
            rise(k)
            fall(k)

        @pl.when(jnp.logical_and(place >= line // 2, place < line - 1))
        def _():
            fall(k)
            rise(k)

    for k in range(chunks):
        mine = turned[side].reshape(line * rows, tokens)
        product = matmul(mine, normed_ref[:, span(k)])
        if k:
            pair_copy(k).wait_send()
            if k + 1 < chunks:
                pair_copy(k + 1).start()
        pair_copy(k).wait_recv()
        there = (came[k] * their_inverse).astype(jnp.bfloat16)
        product = product + matmul(theirs_half[...], there)
        part[k] = product.reshape(part.shape[1:])
        ends(k)
        if k:
            middle(k - 1)
    middle(chunks - 1)

    for k in range(chunks):
        out_ref[:, span(k)] = part[k, place]

        @pl.when(place > 0)
        def _():
            up_copy(k, place).wait_recv()
            out_ref[:, span(k)] = out_ref[:, span(k)] + rising[k, place]

        @pl.when(place < line - 1)
        def _():
            down_copy(k, place).wait_recv()
            out_ref[:, span(k)] = out_ref[:, span(k)] + falling[k, place]

    state_copy().wait_send()
    for b in range(line_bits - 1):
        line_copy(b).wait_send()

    @pl.when((place // (line // 2)) % 2 == 0)
    def _():
        line_copy(line_bits - 1).wait_send()

    give_copy().wait_send()
    for p in range(PIECES):
        grad_copy(p).wait_send()
        for i in range(head_bits):
            for r in held[i]:
                share_copy(r, stages[i], p).wait_send()
    for r in range(1, heads):
        square_copy(r).wait_send()
    root_copy().wait_send()
    for k in range(chunks):
        @pl.loop(place + 1, line)
        def _(d):
            up_copy(k, d).wait_send()

        @pl.loop(0, place)
        def _(d):
            down_copy(k, d).wait_send()


def body(queries, keys, values, level_weights, out_grad):
    tokens, width = queries.shape
    assert tokens == GROUP
    count = lax.axis_size("seq")
    heads = lax.axis_size("head")
    line = count // 2
    line_bits = line.bit_length() - 1
    lanes = D // HEADS
    chunks = width // lanes
    half = chunks // 2
    rows = out_grad.shape[1] // count
    slots = (chunks, line, rows, lanes)
    states = (half, lanes, lanes)
    vmem = pl.BlockSpec(memory_space=pltpu.VMEM)
    smem = pl.BlockSpec(memory_space=pltpu.SMEM)
    away = pl.BlockSpec(memory_space=pltpu.MemorySpace.HBM)
    f32 = jnp.float32
    dma = pltpu.SemaphoreType.DMA
    return pl.pallas_call(
        functools.partial(kernel, line, heads),
        out_shape=(
            jax.ShapeDtypeStruct((tokens, width), jnp.bfloat16),
            jax.ShapeDtypeStruct((rows, width), f32),
        ),
        in_specs=[away, away, away, smem, away],
        out_specs=(vmem, vmem),
        scratch_shapes=[
            pltpu.VMEM(queries.shape, queries.dtype),
            pltpu.VMEM(keys.shape, keys.dtype),
            pltpu.VMEM(values.shape, values.dtype),
            pltpu.VMEM(out_grad.shape, out_grad.dtype),
            pltpu.SemaphoreType.DMA((4,)),
            pltpu.VMEM((chunks, lanes, lanes), f32),
            pltpu.VMEM(states, f32),
            pltpu.VMEM((line_bits, *states), f32),
            pltpu.VMEM((line_bits, *states), f32),
            pltpu.VMEM(states, f32),
            pltpu.VMEM((chunks, lanes, lanes), f32),
            pltpu.VMEM((2, line, rows, tokens), jnp.bfloat16),
            pltpu.VMEM((line // heads, rows, tokens), f32),
            pltpu.VMEM((line, rows, tokens), f32),
            pltpu.VMEM((line * rows, tokens), jnp.bfloat16),
            pltpu.VMEM((chunks, tokens, lanes), f32),
            pltpu.VMEM((chunks, tokens, lanes), f32),
            pltpu.VMEM((8, tokens), f32),
            pltpu.VMEM((heads - 1, 8, tokens), f32),
            pltpu.VMEM((8, tokens), f32),
            pltpu.VMEM((8, tokens), f32),
            pltpu.VMEM(slots, f32),
            pltpu.VMEM(slots, f32),
            pltpu.VMEM(slots, f32),
            dma((2 + line_bits,)),
            dma((2 + line_bits,)),
            dma((heads, PIECES)),
            dma((heads, PIECES)),
            dma((heads - 1,)),
            dma((heads - 1,)),
            dma((1,)),
            dma((1,)),
            dma((chunks,)),
            dma((chunks,)),
            dma((chunks, line)),
            dma((chunks, line)),
            dma((chunks, line)),
            dma((chunks, line)),
        ],
        compiler_params=pltpu.CompilerParams(
            collective_id=0, has_side_effects=True, vmem_limit_bytes=60 << 20
        ),
    )(queries, keys, values, level_weights, out_grad)


def solution(mesh):
    return jax.shard_map(
        body,
        mesh=mesh,
        in_specs=(
            P("seq", "head"),
            P("seq", "head"),
            P("seq", "head"),
            P("head", None),
            P("seq", None),
        ),
        out_specs=(P("seq", "head"), P("seq", "head")),
        check_vma=False,
    )
```

profile of v0, /device:TPU:0, one launch (start us, length us, event | category | flops | bytes accessed | tf_op | source)
XLA Modules:
  0.0 79.5 jit_solution(13621484018244683768)
XLA Ops:
  0.6 75.1 %shard_map.68 = (bf16[512,512]{1,0:T(8,128)(2,1)}, f32[256,512]{1,0:T(8,128)}) custom-call(bf16[512,512]{1,0:T(8,128)(2,1)} %q_in.1, bf16[512,512]{1,0:T(8,128)(2,1)} %k_in.1, bf16[512,512]{1,0:T(8,128)(2,1)} %v_in.1, s32[4,20]{1,0:T(4,128)} %level_ref.1, bf16[512,2048]{1,0:T(8,128)(2,1)} %grad_in.1), custom_call_target="tpu_custom_call" | custom-call | tf_op jit(solution)/shard_map/pallas_call | solution.py:459
  75.7 1.9 %copy.9 = bf16[512,512]{1,0:T(8,128)(2,1)} copy(bf16[512,512]{1,0:T(8,128)(2,1)} %get-tuple-element.4) | data formatting | bytes 1048576
  77.6 1.9 %copy.10 = f32[256,512]{1,0:T(8,128)} copy(f32[256,512]{1,0:T(8,128)} %get-tuple-element.5) | data formatting | bytes 1048576
where the time goes:
time: 79.7 us; the launch traced here: 79.5 us
  Pallas kernels  75.1 us (94%)
  local copies, waits for them, and re-layouts  3.74 us (5%)
    pallas_call x1, Pallas kernels, body(): pl.pallas_call(functools.partial(kernel, line, heads), out_shape=(jax.Sha...  75.1 us
    unnamed x2, local copies, waits for them, and re-layouts  3.74 us

commit v1 on v0

--- a/solution.py
+++ b/solution.py
@@ -459,8 +459,8 @@
     return pl.pallas_call(
         functools.partial(kernel, line, heads),
         out_shape=(
-            jax.ShapeDtypeStruct((tokens, width), jnp.bfloat16),
-            jax.ShapeDtypeStruct((rows, width), f32),
+            pltpu.VMEM((tokens, width), jnp.bfloat16),
+            pltpu.VMEM((rows, width), f32),
         ),
         in_specs=[away, away, away, smem, away],
         out_specs=(vmem, vmem),

time: 79.7 us -> 76.5 us (0.960)
  local copies, waits for them, and re-layouts: 3.74 us -> 1.59 us
  Pallas kernels: 75.1 us -> 74.1 us
    unnamed x2, local copies, waits for them, and re-layouts: 3.74 us -> 1.59 us
    pallas_call x1, Pallas kernels: 75.1 us -> 74.1 us  [body(): pl.pallas_call(functools.partial(kernel, line, heads), out_shape=(pltpu.V...]
where the time goes in v1:
time: 76.5 us; the launch traced here: 76.3 us
  Pallas kernels  74.1 us (97%)
  local copies, waits for them, and re-layouts  1.59 us (2%)
    pallas_call x1, Pallas kernels, body(): pl.pallas_call(functools.partial(kernel, line, heads), out_shape=(pltpu.V...  74.1 us
    unnamed x2, local copies, waits for them, and re-layouts  1.59 us

profile of v1, /device:TPU:0, one launch (start us, length us, event | category | flops | bytes accessed | tf_op | source)
XLA Modules:
  0.0 76.3 jit_solution(6445365282208061259)
XLA Ops:
  0.6 74.1 %shard_map.68 = (bf16[512,512]{1,0:T(8,128)(2,1)S(1)}, f32[256,512]{1,0:T(8,128)S(1)}) custom-call(bf16[512,512]{1,0:T(8,128)(2,1)} %q_in.1, bf16[512,512]{1,0:T(8,128)(2,1)} %k_in.1, bf16[512,512]{1,0:T(8,128)(2,1)} %v_in.1, s32[4,20]{1,0:T(4,128)} %level_ref.1, bf16[512,2048]{1,0:T(8,128)(2,1)} %grad_in.1), custom_call_target="tpu_custom_call" | custom-call | tf_op jit(solution)/shard_map/pallas_call | solution.py:459
  74.8 0.8 %copy.9 = bf16[512,512]{1,0:T(8,128)(2,1)} copy(bf16[512,512]{1,0:T(8,128)(2,1)S(1)} %get-tuple-element.2) | data formatting | bytes 1048576
  75.6 0.8 %copy.10 = f32[256,512]{1,0:T(8,128)} copy(f32[256,512]{1,0:T(8,128)S(1)} %get-tuple-element.3) | data formatting | bytes 1048576

commit v2 on v1

v2 whole, which is shorter than its diff:
```python
import functools

import jax
import jax.numpy as jnp
from jax import lax
from jax.experimental import pallas as pl
from jax.experimental.pallas import tpu as pltpu
from jax.sharding import PartitionSpec as P

D = 2048
HEADS = 16
GROUP = 512
PIECES = 4
STATE_PIECES = 2
SLOT_PIECES = 2
MESH = pl.DeviceIdType.MESH
NT = (((1,), (1,)), ((), ()))
TN = (((0,), (0,)), ((), ()))


def flip(index, mask):
    bit = 1
    while bit <= mask:
        if mask & bit:
            index = index + bit - 2 * bit * ((index // bit) % 2)
        bit *= 2
    return index


def matmul(a, b, dims=(((1,), (0,)), ((), ()))):
    return lax.dot_general(a, b, dims, preferred_element_type=jnp.float32)


def split(x):
    high = x.astype(jnp.bfloat16)
    return high, (x - high.astype(jnp.float32)).astype(jnp.bfloat16)


def kernel(
    line,
    heads,
    q_in,
    k_in,
    v_in,
    level_ref,
    grad_in,
    normed_ref,
    out_ref,
    q_ref,
    k_ref,
    v_ref,
    grad_ref,
    loads,
    state,
    pair_state,
    block,
    line_state,
    give,
    mix,
    turned,
    quarter,
    theirs,
    theirs_half,
    raw,
    came,
    there,
    squares,
    squares_in,
    part,
    rising,
    falling,
    state_send,
    state_recv,
    grad_send,
    grad_recv,
    square_send,
    square_recv,
    pair_send,
    pair_recv,
    up_send,
    up_recv,
    down_send,
    down_recv,
):
    me = lax.axis_index("seq")
    head = lax.axis_index("head")
    place = me // 2
    side = me % 2
    other = flip(me, 1)
    above = me + 2
    below = me - 2
    tokens, width = q_ref.shape
    lanes = D // HEADS
    chunks = width // lanes
    half = chunks // 2
    rows = out_ref.shape[0]
    line_bits = line.bit_length() - 1
    head_bits = heads.bit_length() - 1
    group = line // PIECES
    last = PIECES - 1
    token_share = tokens // heads
    part_rows = rows // SLOT_PIECES
    state_rows = lanes // STATE_PIECES
    stages = list(reversed(range(head_bits)))
    held = [[0]]
    for bit in stages:
        held.append(held[-1] + [r ^ (1 << bit) for r in held[-1]])
    state_parts = [(i, s) for i in range(half) for s in range(STATE_PIECES)]
    scale = lanes ** (-0.5)
    low_end = place == 0
    high_end = place == line - 1

    def span(k):
        return slice(k * lanes, (k + 1) * lanes)

    def columns(k):
        return pl.ds(pl.multiple_of(k * lanes, lanes), lanes)

    def bit_of(b):
        return (place // (1 << b)) % 2

    def ends_block(b):
        return place % (1 << b) == (1 << b) - 1

    mine = place // group
    lower = place < line // 2

    def first_slot(p):
        ordered = jnp.where(lower, mine + PIECES - 1 - p, mine + 1 + p)
        return (ordered % PIECES) * group

    def slots(p):
        return pl.ds(first_slot(p), group)

    pairs = ((k_in, k_ref), (v_in, v_ref), (grad_in, grad_ref), (q_in, q_ref))
    copies = [pltpu.make_async_copy(a, b, loads.at[i]) for i, (a, b) in enumerate(pairs)]
    for copy in copies:
        copy.start()

    barrier = pltpu.get_barrier_semaphore()

    def greet(device):
        pl.semaphore_signal(barrier, inc=1, device_id=device, device_id_type=MESH)

    greet({"seq": other})
    for r in range(1, heads):
        greet({"head": flip(head, r)})
        greet({"seq": other, "head": flip(head, r)})

    @pl.when(place < line - 1)
    def _():
        greet({"seq": above})

    @pl.when(place > 0)
    def _():
        greet({"seq": below})

    def remote(src, dst, send, recv, device):
        return pltpu.make_async_remote_copy(
            src_ref=src,
            dst_ref=dst,
            send_sem=send,
            recv_sem=recv,
            device_id=device,
            device_id_type=MESH,
        )

    def state_span(s):
        return pl.ds(s * state_rows, state_rows)

    def state_copy(i, s):
        number = i * STATE_PIECES + s
        return remote(
            state.at[(1 - side) * half + i, state_span(s)],
            pair_state.at[i, state_span(s)],
            state_send.at[0, number],
            state_recv.at[0, number],
            {"seq": other},
        )

    def line_copy(b, i, s, first=False):
        number = i * STATE_PIECES + s
        return remote(
            (block if first else line_state).at[b, i, state_span(s)],
            line_state.at[b, i, state_span(s)],
            state_send.at[1 + b, number],
            state_recv.at[1 + b, number],
            {"seq": above},
        )

    def give_copy(i, s):
        number = i * STATE_PIECES + s
        return remote(
            give.at[i, state_span(s)],
            mix.at[side * half + i, state_span(s)],
            state_send.at[1 + line_bits, number],
            state_recv.at[1 + line_bits, number],
            {"seq": other},
        )

    def token_span(h):
        return pl.ds(pl.multiple_of(h * token_share, token_share), token_share)

    def grad_copy(p):
        return remote(
            quarter.at[slots(p)],
            theirs.at[slots(p), :, token_span(head)],
            grad_send.at[0, p],
            grad_recv.at[0, p],
            {"seq": other},
        )

    def share_copy(r, bit, p):
        owned = theirs.at[slots(p), :, token_span(flip(head, r))]
        slot = r ^ (1 << bit)
        return remote(
            owned,
            owned,
            grad_send.at[slot, p],
            grad_recv.at[slot, p],
            {"head": flip(head, 1 << bit)},
        )

    def square_copy(r):
        away = r >= heads
        return remote(
            squares.at[pl.ds(0, 1)],
            squares_in.at[r, pl.ds(0, 1)],
            square_send.at[r],
            square_recv.at[r],
            {"seq": other if away else me, "head": flip(head, r % heads)},
        )

    def pair_copy(k, t):
        at = pl.ds(t * (tokens // 2), tokens // 2)
        return remote(
            raw.at[k, at],
            came.at[k, at],
            pair_send.at[k, t],
            pair_recv.at[k, t],
            {"seq": other},
        )

    def part_span(q):
        return pl.ds(q * part_rows, part_rows)

    def up_copy(k, d, q):
        return remote(
            part.at[k, d, part_span(q)],
            rising.at[k, d, part_span(q)],
            up_send.at[k, d, q],
            up_recv.at[k, d, q],
            {"seq": above},
        )

    def down_copy(k, d, q):
        return remote(
            part.at[k, d, part_span(q)],
            falling.at[k, d, part_span(q)],
            down_send.at[k, d, q],
            down_recv.at[k, d, q],
            {"seq": below},
        )

    copies[0].wait()
    copies[1].wait()
    for i in range(half):
        h = (1 - side) * half + i
        state[h] = matmul(k_ref[:, columns(h)], v_ref[:, columns(h)], TN)
        if i == 0:
            peers = 2 * heads - 1 + jnp.where(place > 0, 1, 0) + jnp.where(place < line - 1, 1, 0)
            pl.semaphore_wait(barrier, peers)
        for s in range(STATE_PIECES):
            state_copy(i, s).start()
    for i in range(half):
        h = side * half + i
        state[h] = matmul(k_ref[:, columns(h)], v_ref[:, columns(h)], TN)

    copies[2].wait()
    tile = max(rows, lanes)
    for j in range(grad_ref.shape[1] // tile):
        flat = grad_ref[:, j * tile : (j + 1) * tile].T
        for i in range(tile // rows):
            owner = j * (tile // rows) + i
            turned[owner % 2, owner // 2] = flat[i * rows : (i + 1) * rows]
    quarter[...] = turned[1 - side, :, :, token_span(head)].astype(jnp.float32)
    for p in range(last):
        grad_copy(p).start()

    def forward(i, p):
        for r in held[i]:
            share_copy(r, stages[i], p).start()

    def collect(i, p):
        for r in held[i]:
            share_copy(r, stages[i], p).wait_recv()

    def pass_on(p):
        grad_copy(p).wait_recv()
        forward(0, p)

    def near(h):
        weight = scale * level_ref[h, 0].astype(jnp.float32)
        scores = matmul(q_ref[:, span(h)], k_ref[:, span(h)], NT) * weight
        row = lax.broadcasted_iota(jnp.int32, scores.shape, 0)
        column = lax.broadcasted_iota(jnp.int32, scores.shape, 1)
        probs = jnp.where(column <= row, scores, 0.0).astype(jnp.bfloat16)
        raw[h] = matmul(probs, v_ref[:, span(h)])

    def level(i, number):
        return level_ref[side * half + i, number].astype(jnp.float32)

    for b in range(line_bits):

        @pl.when(bit_of(b) == 0)
        def _():
            line_state[b] = jnp.zeros(line_state.shape[1:], jnp.float32)

    copies[3].wait()
    for i, s in state_parts:
        at = (i, state_span(s))
        state_copy(i, s).wait_recv()
        block[0, *at] = state[side * half + i, state_span(s)] + pair_state[*at]

        @pl.when(bit_of(0) == 0)
        def _():
            line_copy(0, i, s, True).start()

    @pl.when(high_end)
    def _():
        for h in range(chunks):
            near(h)
        pass_on(0)

    for i, s in state_parts:
        at = (i, state_span(s))
        for b in range(line_bits):

            @pl.when(bit_of(b) == 1)
            def _():
                line_copy(b, i, s).wait_recv()

            if b:

                @pl.when(jnp.logical_and(bit_of(b) == 1, jnp.logical_not(ends_block(b))))
                def _():
                    line_copy(b, i, s).start()

            if b + 1 < line_bits:
                block[b + 1, *at] = block[b, *at] + line_state[b, *at]

                @pl.when(jnp.logical_and(bit_of(b + 1) == 0, ends_block(b + 1)))
                def _():
                    line_copy(b + 1, i, s, True).start()

        far = jnp.zeros((state_rows, lanes), jnp.float32)
        for b in range(line_bits):
            far = far + (level(i, 2 + b) * bit_of(b).astype(jnp.float32)) * line_state[b, *at]
        first = level(i, 1)
        right = side.astype(jnp.float32)
        mix[side * half + i, state_span(s)] = far + (first * right) * pair_state[*at]
        give[*at] = far + (first * (1.0 - right)) * state[side * half + i, state_span(s)]
        give_copy(i, s).start()

    @pl.when(jnp.logical_not(high_end))
    def _():
        for h in range(chunks):
            near(h)
            if h == 0:
                pass_on(0)

    for p in range(1, last):
        pass_on(p)

    total = jnp.zeros((tokens, lanes), jnp.float32)
    for h in range(chunks):

        @pl.when(side != h // half)
        def _():
            for s in range(STATE_PIECES):
                give_copy(h % half, s).wait_recv()

        high, low = split(mix[h])
        query = q_ref[:, span(h)]
        value = raw[h] + scale * (matmul(query, high) + matmul(query, low))
        raw[h] = value
        if h == 0:
            pair_copy(0, 0).start()
        total = total + value * value
    ones = jnp.ones((8, lanes), jnp.bfloat16)
    high, low = split(total)
    squares[...] = matmul(ones, high, NT) + matmul(ones, low, NT)
    for r in range(1, 2 * heads):
        square_copy(r).start()
    pair_copy(0, 1).start()
    for p in range(last):
        collect(0, p)
        for i in range(1, head_bits):
            if i > 1:
                collect(i - 1, p)
            forward(i, p)
    for t in range(2):
        pair_copy(1, t).start()
    grad_copy(last).start()
    for k in range(2, chunks):
        for t in range(2):
            pair_copy(k, t).start()

    def inverse_of(whole):
        root = lax.rsqrt(whole / D + 1e-06)
        return jnp.broadcast_to(root, (8, tokens)).T[:, :1]

    whole = squares[0:1]
    for r in range(1, heads):
        square_copy(r).wait_recv()
        whole = whole + squares_in[r, 0:1]
    inverse = inverse_of(whole)
    for h in range(chunks):
        normed_ref[:, span(h)] = (raw[h] * inverse).astype(jnp.bfloat16)

    def arrive(p):
        collect(head_bits - 1, p)
        theirs_half[slots(p)] = theirs[slots(p)].astype(jnp.bfloat16)

    for p in range(last):
        arrive(p)

    def product(k, p):
        flat = (group * rows, tokens)
        value = matmul(turned[side, slots(p)].reshape(flat), normed_ref[:, span(k)])
        value = value + matmul(theirs_half[slots(p)].reshape(flat), there[k])
        part[k, slots(p)] = value.reshape(group, rows, lanes)
        start = first_slot(p)

        @pl.when(high_end)
        def _():
            @pl.loop(0, group)
            def _(i):
                @pl.when(start + i < place)
                def _():
                    for q in range(SLOT_PIECES):
                        down_copy(k, start + i, q).start()

        @pl.when(low_end)
        def _():
            @pl.loop(0, group)
            def _(i):
                @pl.when(start + i > place)
                def _():
                    for q in range(SLOT_PIECES):
                        up_copy(k, start + i, q).start()

    def rise(k):
        @pl.loop(0, line - 1 - place)
        def _(i):
            d = line - 1 - i
            for q in range(SLOT_PIECES):
                up_copy(k, d, q).wait_recv()
                part[k, d, part_span(q)] = part[k, d, part_span(q)] + rising[k, d, part_span(q)]
                up_copy(k, d, q).start()

    def fall(k):
        @pl.loop(0, place)
        def _(d):
            for q in range(SLOT_PIECES):
                down_copy(k, d, q).wait_recv()
                part[k, d, part_span(q)] = part[k, d, part_span(q)] + falling[k, d, part_span(q)]
                down_copy(k, d, q).start()

    inner = jnp.logical_and(place > 0, place < line - 1)

    def nearer(k):
        @pl.when(jnp.logical_and(inner, lower))
        def _():
            rise(k)

        @pl.when(jnp.logical_and(inner, jnp.logical_not(lower)))
        def _():
            fall(k)

    def farther(k):
        @pl.when(jnp.logical_and(inner, lower))
        def _():
            fall(k)

        @pl.when(jnp.logical_and(inner, jnp.logical_not(lower)))
        def _():
            rise(k)

    alone = group == 1
    whole = jnp.zeros((1, tokens), jnp.float32)
    for r in range(heads, 2 * heads):
        square_copy(r).wait_recv()
        whole = whole + squares_in[r, 0:1]
    their_inverse = inverse_of(whole)
    for k in range(chunks):
        for t in range(2):
            pair_copy(k, t).wait_recv()
        there[k] = (came[k] * their_inverse).astype(jnp.bfloat16)
        for p in range(last):
            product(k, p)
        if k == 0 and alone:
            nearer(0)
        if k == 1:
            if alone:
                farther(0)
            pass_on(last)
            collect(0, last)
            for i in range(1, head_bits):
                if i > 1:
                    collect(i - 1, last)
                forward(i, last)
            arrive(last)
            product(0, last)
            product(1, last)
            if not alone:
                nearer(0)
                farther(0)
        if k > 1:
            product(k, last)
            nearer(k - 1)
            farther(k - 1)
    nearer(chunks - 1)
    farther(chunks - 1)

    for i, s in state_parts:
        state_copy(i, s).wait_send()
        for b in range(line_bits):

            @pl.when(jnp.logical_xor(bit_of(b) == 1, ends_block(b)))
            def _():
                line_copy(b, i, s).wait_send()

        give_copy(i, s).wait_send()
    for p in range(PIECES):
        grad_copy(p).wait_send()
        for i in range(head_bits):
            for r in held[i]:
                share_copy(r, stages[i], p).wait_send()
    for r in range(1, 2 * heads):
        square_copy(r).wait_send()
    for k in range(chunks):
        for t in range(2):
            pair_copy(k, t).wait_send()

    def settle(k):
        for q in range(SLOT_PIECES):

            @pl.loop(place + 1, line)
            def _(d):
                up_copy(k, d, q).wait_send()

            @pl.loop(0, place)
            def _(d):
                down_copy(k, d, q).wait_send()

    for k in range(chunks):
        if k:
            settle(k - 1)
        out_ref[:, span(k)] = part[k, place]

        @pl.when(place > 0)
        def _():
            for q in range(SLOT_PIECES):
                up_copy(k, place, q).wait_recv()
            out_ref[:, span(k)] = out_ref[:, span(k)] + rising[k, place]

        @pl.when(place < line - 1)
        def _():
            for q in range(SLOT_PIECES):
                down_copy(k, place, q).wait_recv()
            out_ref[:, span(k)] = out_ref[:, span(k)] + falling[k, place]

    settle(chunks - 1)


def body(queries, keys, values, level_weights, out_grad):
    tokens, width = queries.shape
    assert tokens == GROUP
    count = lax.axis_size("seq")
    heads = lax.axis_size("head")
    line = count // 2
    line_bits = line.bit_length() - 1
    lanes = D // HEADS
    chunks = width // lanes
    half = chunks // 2
    rows = out_grad.shape[1] // count
    slots = (chunks, line, rows, lanes)
    states = (half, lanes, lanes)
    vmem = pl.BlockSpec(memory_space=pltpu.VMEM)
    smem = pl.BlockSpec(memory_space=pltpu.SMEM)
    away = pl.BlockSpec(memory_space=pltpu.MemorySpace.HBM)
    f32 = jnp.float32
    dma = pltpu.SemaphoreType.DMA
    return pl.pallas_call(
        functools.partial(kernel, line, heads),
        out_shape=(
            pltpu.VMEM((tokens, width), jnp.bfloat16),
            pltpu.VMEM((rows, width), f32),
        ),
        in_specs=[away, away, away, smem, away],
        out_specs=(vmem, vmem),
        scratch_shapes=[
            pltpu.VMEM(queries.shape, queries.dtype),
            pltpu.VMEM(keys.shape, keys.dtype),
            pltpu.VMEM(values.shape, values.dtype),
            pltpu.VMEM(out_grad.shape, out_grad.dtype),
            pltpu.SemaphoreType.DMA((4,)),
            pltpu.VMEM((chunks, lanes, lanes), f32),
            pltpu.VMEM(states, f32),
            pltpu.VMEM((line_bits, *states), f32),
            pltpu.VMEM((line_bits, *states), f32),
            pltpu.VMEM(states, f32),
            pltpu.VMEM((chunks, lanes, lanes), f32),
            pltpu.VMEM((2, line, rows, tokens), jnp.bfloat16),
            pltpu.VMEM((line, rows, tokens // heads), f32),
            pltpu.VMEM((line, rows, tokens), f32),
            pltpu.VMEM((line, rows, tokens), jnp.bfloat16),
            pltpu.VMEM((chunks, tokens, lanes), f32),
            pltpu.VMEM((chunks, tokens, lanes), f32),
            pltpu.VMEM((chunks, tokens, lanes), jnp.bfloat16),
            pltpu.VMEM((8, tokens), f32),
            pltpu.VMEM((2 * heads, 8, tokens), f32),
            pltpu.VMEM(slots, f32),
            pltpu.VMEM(slots, f32),
            pltpu.VMEM(slots, f32),
            dma((2 + line_bits, half * STATE_PIECES)),
            dma((2 + line_bits, half * STATE_PIECES)),
            dma((heads, PIECES)),
            dma((heads, PIECES)),
            dma((2 * heads,)),
            dma((2 * heads,)),
            dma((chunks, 2)),
            dma((chunks, 2)),
            dma((chunks, line, SLOT_PIECES)),
            dma((chunks, line, SLOT_PIECES)),
            dma((chunks, line, SLOT_PIECES)),
            dma((chunks, line, SLOT_PIECES)),
        ],
        compiler_params=pltpu.CompilerParams(
            collective_id=0, has_side_effects=True, vmem_limit_bytes=60 << 20
        ),
    )(queries, keys, values, level_weights, out_grad)


def solution(mesh):
    return jax.shard_map(
        body,
        mesh=mesh,
        in_specs=(
            P("seq", "head"),
            P("seq", "head"),
            P("seq", "head"),
            P("head", None),
            P("seq", None),
        ),
        out_specs=(P("seq", "head"), P("seq", "head")),
        check_vma=False,
    )
```

time: 76.5 us -> 71.1 us (0.929)
  Pallas kernels: 74.1 us -> 68.7 us
    pallas_call x1, Pallas kernels: 74.1 us -> 68.7 us  [body(): pl.pallas_call(functools.partial(kernel, line, heads), out_shape=(pltpu.V...]
where the time goes in v2:
time: 71.1 us; the launch traced here: 70.9 us
  Pallas kernels  68.7 us (97%)
  local copies, waits for them, and re-layouts  1.59 us (2%)
    pallas_call x1, Pallas kernels, body(): pl.pallas_call(functools.partial(kernel, line, heads), out_shape=(pltpu.V...  68.7 us
    unnamed x2, local copies, waits for them, and re-layouts  1.59 us

profile of v2, /device:TPU:0, one launch (start us, length us, event | category | flops | bytes accessed | tf_op | source)
XLA Modules:
  0.0 70.9 jit_solution(1641065275640804564)
XLA Ops:
  0.6 68.7 %shard_map.68 = (bf16[512,512]{1,0:T(8,128)(2,1)S(1)}, f32[256,512]{1,0:T(8,128)S(1)}) custom-call(bf16[512,512]{1,0:T(8,128)(2,1)} %q_in.1, bf16[512,512]{1,0:T(8,128)(2,1)} %k_in.1, bf16[512,512]{1,0:T(8,128)(2,1)} %v_in.1, s32[4,20]{1,0:T(4,128)} %level_ref.1, bf16[512,2048]{1,0:T(8,128)(2,1)} %grad_in.1), custom_call_target="tpu_custom_call" | custom-call | tf_op jit(solution)/shard_map/pallas_call | solution.py:595
  69.4 0.8 %copy.9 = bf16[512,512]{1,0:T(8,128)(2,1)} copy(bf16[512,512]{1,0:T(8,128)(2,1)S(1)} %get-tuple-element.2) | data formatting | bytes 1048576
  70.2 0.8 %copy.10 = f32[256,512]{1,0:T(8,128)} copy(f32[256,512]{1,0:T(8,128)S(1)} %get-tuple-element.3) | data formatting | bytes 1048576

commit v3 on v2

--- a/solution.py
+++ b/solution.py
@@ -12,6 +12,7 @@
 GROUP = 512
 PIECES = 4
 STATE_PIECES = 2
+FIRST_SLOT_PIECES = 1
 SLOT_PIECES = 2
 MESH = pl.DeviceIdType.MESH
 NT = (((1,), (1,)), ((), ()))
@@ -42,7 +43,7 @@
     q_in,
     k_in,
     v_in,
-    level_ref,
+    level_in,
     grad_in,
     normed_ref,
     out_ref,
@@ -50,6 +51,7 @@
     k_ref,
     v_ref,
     grad_ref,
+    level_ref,
     loads,
     state,
     pair_state,
@@ -77,10 +79,8 @@
     square_recv,
     pair_send,
     pair_recv,
-    up_send,
-    up_recv,
-    down_send,
-    down_recv,
+    slot_send,
+    slot_recv,
 ):
     me = lax.axis_index("seq")
     head = lax.axis_index("head")
@@ -98,8 +98,11 @@
     head_bits = heads.bit_length() - 1
     group = line // PIECES
     last = PIECES - 1
+    bulk = [(p, 0, rows) for p in range(last - 1)]
+    bulk += [(last - 1, 0, rows // 2), (last - 1, rows // 2, rows // 2)]
+    bulk += [(last, 0, rows)]
+    late, final = len(bulk) - 2, len(bulk) - 1
     token_share = tokens // heads
-    part_rows = rows // SLOT_PIECES
     state_rows = lanes // STATE_PIECES
     stages = list(reversed(range(head_bits)))
     held = [[0]]
@@ -132,7 +135,7 @@
     def slots(p):
         return pl.ds(first_slot(p), group)
 
-    pairs = ((k_in, k_ref), (v_in, v_ref), (grad_in, grad_ref), (q_in, q_ref))
+    pairs = ((k_in, k_ref), (v_in, v_ref), (grad_in, grad_ref), (q_in, q_ref), (level_in, level_ref))
     copies = [pltpu.make_async_copy(a, b, loads.at[i]) for i, (a, b) in enumerate(pairs)]
     for copy in copies:
         copy.start()
@@ -173,7 +176,7 @@
         return remote(
             state.at[(1 - side) * half + i, state_span(s)],
             pair_state.at[i, state_span(s)],
-            state_send.at[0, number],
+            state_send.at[0],
             state_recv.at[0, number],
             {"seq": other},
         )
@@ -183,7 +186,7 @@
         return remote(
             (block if first else line_state).at[b, i, state_span(s)],
             line_state.at[b, i, state_span(s)],
-            state_send.at[1 + b, number],
+            state_send.at[1 + b],
             state_recv.at[1 + b, number],
             {"seq": above},
         )
@@ -193,7 +196,7 @@
         return remote(
             give.at[i, state_span(s)],
             mix.at[side * half + i, state_span(s)],
-            state_send.at[1 + line_bits, number],
+            state_send.at[1 + line_bits],
             state_recv.at[1 + line_bits, number],
             {"seq": other},
         )
@@ -201,23 +204,25 @@
     def token_span(h):
         return pl.ds(pl.multiple_of(h * token_share, token_share), token_share)
 
-    def grad_copy(p):
-        return remote(
-            quarter.at[slots(p)],
-            theirs.at[slots(p), :, token_span(head)],
-            grad_send.at[0, p],
-            grad_recv.at[0, p],
+    def grad_copy(e):
+        p, start, size = bulk[e]
+        return remote(
+            quarter.at[slots(p), pl.ds(start, size)],
+            theirs.at[slots(p), pl.ds(start, size), token_span(head)],
+            grad_send.at[0],
+            grad_recv.at[0, e],
             {"seq": other},
         )
 
-    def share_copy(r, bit, p):
-        owned = theirs.at[slots(p), :, token_span(flip(head, r))]
+    def share_copy(r, bit, e):
+        p, start, size = bulk[e]
+        owned = theirs.at[slots(p), pl.ds(start, size), token_span(flip(head, r))]
         slot = r ^ (1 << bit)
         return remote(
             owned,
             owned,
-            grad_send.at[slot, p],
-            grad_recv.at[slot, p],
+            grad_send.at[0],
+            grad_recv.at[slot, e],
             {"head": flip(head, 1 << bit)},
         )
 
@@ -226,39 +231,50 @@
         return remote(
             squares.at[pl.ds(0, 1)],
             squares_in.at[r, pl.ds(0, 1)],
-            square_send.at[r],
+            square_send.at[0],
             square_recv.at[r],
             {"seq": other if away else me, "head": flip(head, r % heads)},
         )
 
     def pair_copy(k, t):
-        at = pl.ds(t * (tokens // 2), tokens // 2)
+        size = tokens // pair_parts(k)
+        at = pl.ds(t * size, size)
         return remote(
             raw.at[k, at],
             came.at[k, at],
-            pair_send.at[k, t],
-            pair_recv.at[k, t],
+            pair_send.at[0],
+            pair_recv.at[k + 1 if k else t],
             {"seq": other},
         )
 
-    def part_span(q):
-        return pl.ds(q * part_rows, part_rows)
+    def pair_parts(k):
+        return 1 if k else 2
+
+    def slot_parts(k):
+        return SLOT_PIECES if k == chunks - 1 else FIRST_SLOT_PIECES
+
+    def part_span(k, q):
+        size = rows // slot_parts(k)
+        return pl.ds(q * size, size)
+
+    def lane_of(k, q):
+        return k * FIRST_SLOT_PIECES + q
 
     def up_copy(k, d, q):
         return remote(
-            part.at[k, d, part_span(q)],
-            rising.at[k, d, part_span(q)],
-            up_send.at[k, d, q],
-            up_recv.at[k, d, q],
+            part.at[k, d, part_span(k, q)],
+            rising.at[k, d, part_span(k, q)],
+            slot_send.at[0],
+            slot_recv.at[lane_of(k, q), d],
             {"seq": above},
         )
 
     def down_copy(k, d, q):
         return remote(
-            part.at[k, d, part_span(q)],
-            falling.at[k, d, part_span(q)],
-            down_send.at[k, d, q],
-            down_recv.at[k, d, q],
+            part.at[k, d, part_span(k, q)],
+            falling.at[k, d, part_span(k, q)],
+            slot_send.at[0],
+            slot_recv.at[lane_of(k, q), (d + line) % (line + 1)],
             {"seq": below},
         )
 
@@ -284,8 +300,8 @@
             owner = j * (tile // rows) + i
             turned[owner % 2, owner // 2] = flat[i * rows : (i + 1) * rows]
     quarter[...] = turned[1 - side, :, :, token_span(head)].astype(jnp.float32)
-    for p in range(last):
-        grad_copy(p).start()
+    for e in range(late):
+        grad_copy(e).start()
 
     def forward(i, p):
         for r in held[i]:
@@ -317,6 +333,7 @@
             line_state[b] = jnp.zeros(line_state.shape[1:], jnp.float32)
 
     copies[3].wait()
+    copies[4].wait()
     for i, s in state_parts:
         at = (i, state_span(s))
         state_copy(i, s).wait_recv()
@@ -362,6 +379,8 @@
         give[*at] = far + (first * (1.0 - right)) * state[side * half + i, state_span(s)]
         give_copy(i, s).start()
 
+    grad_copy(late).start()
+
     @pl.when(jnp.logical_not(high_end))
     def _():
         for h in range(chunks):
@@ -369,8 +388,8 @@
             if h == 0:
                 pass_on(0)
 
-    for p in range(1, last):
-        pass_on(p)
+    for e in range(1, late):
+        pass_on(e)
 
     total = jnp.zeros((tokens, lanes), jnp.float32)
     for h in range(chunks):
@@ -393,18 +412,17 @@
     for r in range(1, 2 * heads):
         square_copy(r).start()
     pair_copy(0, 1).start()
-    for p in range(last):
-        collect(0, p)
+    pass_on(late)
+    for e in range(final):
+        collect(0, e)
         for i in range(1, head_bits):
             if i > 1:
-                collect(i - 1, p)
-            forward(i, p)
-    for t in range(2):
-        pair_copy(1, t).start()
-    grad_copy(last).start()
+                collect(i - 1, e)
+            forward(i, e)
+    pair_copy(1, 0).start()
+    grad_copy(final).start()
     for k in range(2, chunks):
-        for t in range(2):
-            pair_copy(k, t).start()
+        pair_copy(k, 0).start()
 
     def inverse_of(whole):
         root = lax.rsqrt(whole / D + 1e-06)
@@ -419,7 +437,9 @@
         normed_ref[:, span(h)] = (raw[h] * inverse).astype(jnp.bfloat16)
 
     def arrive(p):
-        collect(head_bits - 1, p)
+        for e in range(len(bulk)):
+            if bulk[e][0] == p:
+                collect(head_bits - 1, e)
         theirs_half[slots(p)] = theirs[slots(p)].astype(jnp.bfloat16)
 
     for p in range(last):
@@ -438,7 +458,7 @@
             def _(i):
                 @pl.when(start + i < place)
                 def _():
-                    for q in range(SLOT_PIECES):
+                    for q in range(slot_parts(k)):
                         down_copy(k, start + i, q).start()
 
         @pl.when(low_end)
@@ -447,24 +467,24 @@
             def _(i):
                 @pl.when(start + i > place)
                 def _():
-                    for q in range(SLOT_PIECES):
+                    for q in range(slot_parts(k)):
                         up_copy(k, start + i, q).start()
 
     def rise(k):
         @pl.loop(0, line - 1 - place)
         def _(i):
             d = line - 1 - i
-            for q in range(SLOT_PIECES):
+            for q in range(slot_parts(k)):
                 up_copy(k, d, q).wait_recv()
-                part[k, d, part_span(q)] = part[k, d, part_span(q)] + rising[k, d, part_span(q)]
+                part[k, d, part_span(k, q)] = part[k, d, part_span(k, q)] + rising[k, d, part_span(k, q)]
                 up_copy(k, d, q).start()
 
     def fall(k):
         @pl.loop(0, place)
         def _(d):
-            for q in range(SLOT_PIECES):
+            for q in range(slot_parts(k)):
                 down_copy(k, d, q).wait_recv()
-                part[k, d, part_span(q)] = part[k, d, part_span(q)] + falling[k, d, part_span(q)]
+                part[k, d, part_span(k, q)] = part[k, d, part_span(k, q)] + falling[k, d, part_span(k, q)]
                 down_copy(k, d, q).start()
 
     inner = jnp.logical_and(place > 0, place < line - 1)
@@ -494,7 +514,7 @@
         whole = whole + squares_in[r, 0:1]
     their_inverse = inverse_of(whole)
     for k in range(chunks):
-        for t in range(2):
+        for t in range(pair_parts(k)):
             pair_copy(k, t).wait_recv()
         there[k] = (came[k] * their_inverse).astype(jnp.bfloat16)
         for p in range(last):
@@ -504,12 +524,12 @@
         if k == 1:
             if alone:
                 farther(0)
-            pass_on(last)
-            collect(0, last)
+            pass_on(final)
+            collect(0, final)
             for i in range(1, head_bits):
                 if i > 1:
-                    collect(i - 1, last)
-                forward(i, last)
+                    collect(i - 1, final)
+                forward(i, final)
             arrive(last)
             product(0, last)
             product(1, last)
@@ -523,55 +543,37 @@
     nearer(chunks - 1)
     farther(chunks - 1)
 
-    for i, s in state_parts:
-        state_copy(i, s).wait_send()
-        for b in range(line_bits):
-
-            @pl.when(jnp.logical_xor(bit_of(b) == 1, ends_block(b)))
-            def _():
-                line_copy(b, i, s).wait_send()
-
-        give_copy(i, s).wait_send()
-    for p in range(PIECES):
-        grad_copy(p).wait_send()
-        for i in range(head_bits):
-            for r in held[i]:
-                share_copy(r, stages[i], p).wait_send()
-    for r in range(1, 2 * heads):
-        square_copy(r).wait_send()
+    def drain(ref, sem):
+        remote(ref, ref, sem, sem, {"seq": other}).wait_send()
+
+    drain(pair_state, state_send.at[0])
+    for b in range(line_bits):
+
+        @pl.when(jnp.logical_xor(bit_of(b) == 1, ends_block(b)))
+        def _():
+            drain(block.at[b], state_send.at[1 + b])
+
+    drain(give, state_send.at[1 + line_bits])
+    drain(theirs, grad_send.at[0])
+    drain(squares_in.at[pl.ds(1, 2 * heads - 1), pl.ds(0, 1)], square_send.at[0])
+    drain(raw, pair_send.at[0])
+
     for k in range(chunks):
-        for t in range(2):
-            pair_copy(k, t).wait_send()
-
-    def settle(k):
-        for q in range(SLOT_PIECES):
-
-            @pl.loop(place + 1, line)
-            def _(d):
-                up_copy(k, d, q).wait_send()
-
-            @pl.loop(0, place)
-            def _(d):
-                down_copy(k, d, q).wait_send()
-
-    for k in range(chunks):
-        if k:
-            settle(k - 1)
         out_ref[:, span(k)] = part[k, place]
 
         @pl.when(place > 0)
         def _():
-            for q in range(SLOT_PIECES):
+            for q in range(slot_parts(k)):
                 up_copy(k, place, q).wait_recv()
             out_ref[:, span(k)] = out_ref[:, span(k)] + rising[k, place]
 
         @pl.when(place < line - 1)
         def _():
-            for q in range(SLOT_PIECES):
+            for q in range(slot_parts(k)):
                 down_copy(k, place, q).wait_recv()
             out_ref[:, span(k)] = out_ref[:, span(k)] + falling[k, place]
 
-    settle(chunks - 1)
+    drain(part.at[:, pl.ds(0, line - 1)], slot_send.at[0])
 
 
 def body(queries, keys, values, level_weights, out_grad):
@@ -588,7 +590,6 @@
     slots = (chunks, line, rows, lanes)
     states = (half, lanes, lanes)
     vmem = pl.BlockSpec(memory_space=pltpu.VMEM)
-    smem = pl.BlockSpec(memory_space=pltpu.SMEM)
     away = pl.BlockSpec(memory_space=pltpu.MemorySpace.HBM)
     f32 = jnp.float32
     dma = pltpu.SemaphoreType.DMA
@@ -598,14 +599,15 @@
             pltpu.VMEM((tokens, width), jnp.bfloat16),
             pltpu.VMEM((rows, width), f32),
         ),
-        in_specs=[away, away, away, smem, away],
+        in_specs=[away] * 5,
         out_specs=(vmem, vmem),
         scratch_shapes=[
             pltpu.VMEM(queries.shape, queries.dtype),
             pltpu.VMEM(keys.shape, keys.dtype),
             pltpu.VMEM(values.shape, values.dtype),
             pltpu.VMEM(out_grad.shape, out_grad.dtype),
-            pltpu.SemaphoreType.DMA((4,)),
+            pltpu.SMEM(level_weights.shape, level_weights.dtype),
+            dma((5,)),
             pltpu.VMEM((chunks, lanes, lanes), f32),
             pltpu.VMEM(states, f32),
             pltpu.VMEM((line_bits, *states), f32),
@@ -624,18 +626,16 @@
             pltpu.VMEM(slots, f32),
             pltpu.VMEM(slots, f32),
             pltpu.VMEM(slots, f32),
+            dma((2 + line_bits,)),
             dma((2 + line_bits, half * STATE_PIECES)),
-            dma((2 + line_bits, half * STATE_PIECES)),
-            dma((heads, PIECES)),
-            dma((heads, PIECES)),
+            dma((1,)),
+            dma((heads, PIECES + 1)),
+            dma((1,)),
             dma((2 * heads,)),
-            dma((2 * heads,)),
-            dma((chunks, 2)),
-            dma((chunks, 2)),
-            dma((chunks, line, SLOT_PIECES)),
-            dma((chunks, line, SLOT_PIECES)),
-            dma((chunks, line, SLOT_PIECES)),
-            dma((chunks, line, SLOT_PIECES)),
+            dma((1,)),
+            dma((chunks + 1,)),
+            dma((1,)),
+            dma(((chunks - 1) * FIRST_SLOT_PIECES + SLOT_PIECES, line + 1)),
         ],
         compiler_params=pltpu.CompilerParams(
             collective_id=0, has_side_effects=True, vmem_limit_bytes=60 << 20

time: 71.1 us -> 69.2 us (0.973)
  Pallas kernels: 68.7 us -> 66.8 us
    pallas_call x1, Pallas kernels: 68.7 us -> 66.8 us  [body(): pl.pallas_call(functools.partial(kernel, line, heads), out_shape=(pltpu.V...]
where the time goes in v3:
time: 69.2 us; the launch traced here: 69 us
  Pallas kernels  66.8 us (97%)
  local copies, waits for them, and re-layouts  1.59 us (2%)
    pallas_call x1, Pallas kernels, body(): pl.pallas_call(functools.partial(kernel, line, heads), out_shape=(pltpu.V...  66.8 us
    unnamed x2, local copies, waits for them, and re-layouts  1.59 us

profile of v3, /device:TPU:0, one launch (start us, length us, event | category | flops | bytes accessed | tf_op | source)
XLA Modules:
  0.0 69.0 jit_solution(1209998259429408868)
XLA Ops:
  0.6 66.8 %shard_map.68 = (bf16[512,512]{1,0:T(8,128)(2,1)S(1)}, f32[256,512]{1,0:T(8,128)S(1)}) custom-call(bf16[512,512]{1,0:T(8,128)(2,1)} %q_in.1, bf16[512,512]{1,0:T(8,128)(2,1)} %k_in.1, bf16[512,512]{1,0:T(8,128)(2,1)} %v_in.1, s32[4,20]{1,0:T(4,128)} %level_in.1, bf16[512,2048]{1,0:T(8,128)(2,1)} %grad_in.1), custom_call_target="tpu_custom_call" | custom-call | tf_op jit(solution)/shard_map/pallas_call | solution.py:596
  67.4 0.8 %copy.9 = bf16[512,512]{1,0:T(8,128)(2,1)} copy(bf16[512,512]{1,0:T(8,128)(2,1)S(1)} %get-tuple-element.2) | data formatting | bytes 1048576
  68.2 0.8 %copy.10 = f32[256,512]{1,0:T(8,128)} copy(f32[256,512]{1,0:T(8,128)S(1)} %get-tuple-element.3) | data formatting | bytes 1048576

commit v4 on v3

--- a/solution.py
+++ b/solution.py
@@ -13,7 +13,8 @@
 PIECES = 4
 STATE_PIECES = 2
 FIRST_SLOT_PIECES = 1
-SLOT_PIECES = 2
+SLOT_PIECES = 4
+SUBLANES = 8
 MESH = pl.DeviceIdType.MESH
 NT = (((1,), (1,)), ((), ()))
 TN = (((0,), (0,)), ((), ()))
@@ -35,6 +36,10 @@
 def split(x):
     high = x.astype(jnp.bfloat16)
     return high, (x - high.astype(jnp.float32)).astype(jnp.bfloat16)
+
+
+def last_parts(rows):
+    return max(1, min(SLOT_PIECES, rows // SUBLANES))
 
 
 def kernel(
@@ -251,7 +256,7 @@
         return 1 if k else 2
 
     def slot_parts(k):
-        return SLOT_PIECES if k == chunks - 1 else FIRST_SLOT_PIECES
+        return last_parts(rows) if k == chunks - 1 else FIRST_SLOT_PIECES
 
     def part_span(k, q):
         size = rows // slot_parts(k)
@@ -379,8 +384,6 @@
         give[*at] = far + (first * (1.0 - right)) * state[side * half + i, state_span(s)]
         give_copy(i, s).start()
 
-    grad_copy(late).start()
-
     @pl.when(jnp.logical_not(high_end))
     def _():
         for h in range(chunks):
@@ -412,8 +415,8 @@
     for r in range(1, 2 * heads):
         square_copy(r).start()
     pair_copy(0, 1).start()
-    pass_on(late)
-    for e in range(final):
+    grad_copy(late).start()
+    for e in range(late):
         collect(0, e)
         for i in range(1, head_bits):
             if i > 1:
@@ -436,13 +439,21 @@
     for h in range(chunks):
         normed_ref[:, span(h)] = (raw[h] * inverse).astype(jnp.bfloat16)
 
+    def gather(e):
+        pass_on(e)
+        collect(0, e)
+        for i in range(1, head_bits):
+            if i > 1:
+                collect(i - 1, e)
+            forward(i, e)
+
     def arrive(p):
         for e in range(len(bulk)):
             if bulk[e][0] == p:
                 collect(head_bits - 1, e)
         theirs_half[slots(p)] = theirs[slots(p)].astype(jnp.bfloat16)
 
-    for p in range(last):
+    for p in range(last - 1):
         arrive(p)
 
     def product(k, p):
@@ -518,18 +529,16 @@
             pair_copy(k, t).wait_recv()
         there[k] = (came[k] * their_inverse).astype(jnp.bfloat16)
         for p in range(last):
+            if k == 0 and p == last - 1:
+                gather(late)
+                arrive(p)
             product(k, p)
         if k == 0 and alone:
             nearer(0)
         if k == 1:
             if alone:
                 farther(0)
-            pass_on(final)
-            collect(0, final)
-            for i in range(1, head_bits):
-                if i > 1:
-                    collect(i - 1, final)
-                forward(i, final)
+            gather(final)
             arrive(last)
             product(0, last)
             product(1, last)
@@ -635,7 +644,7 @@
             dma((1,)),
             dma((chunks + 1,)),
             dma((1,)),
-            dma(((chunks - 1) * FIRST_SLOT_PIECES + SLOT_PIECES, line + 1)),
+            dma(((chunks - 1) * FIRST_SLOT_PIECES + last_parts(rows), line + 1)),
         ],
         compiler_params=pltpu.CompilerParams(
             collective_id=0, has_side_effects=True, vmem_limit_bytes=60 << 20

time: 69.2 us -> 68.1 us (0.984)
  Pallas kernels: 66.8 us -> 65.8 us
    pallas_call x1, Pallas kernels: 66.8 us -> 65.8 us  [body(): pl.pallas_call(functools.partial(kernel, line, heads), out_shape=(pltpu.V...]
where the time goes in v4:
time: 68.1 us; the launch traced here: 68 us
  Pallas kernels  65.8 us (97%)
  local copies, waits for them, and re-layouts  1.59 us (2%)
    pallas_call x1, Pallas kernels, body(): pl.pallas_call(functools.partial(kernel, line, heads), out_shape=(pltpu.V...  65.8 us
    unnamed x2, local copies, waits for them, and re-layouts  1.59 us

profile of v4, /device:TPU:0, one launch (start us, length us, event | category | flops | bytes accessed | tf_op | source)
XLA Modules:
  0.0 68.0 jit_solution(9644773842851309098)
XLA Ops:
  0.6 65.8 %shard_map.68 = (bf16[512,512]{1,0:T(8,128)(2,1)S(1)}, f32[256,512]{1,0:T(8,128)S(1)}) custom-call(bf16[512,512]{1,0:T(8,128)(2,1)} %q_in.1, bf16[512,512]{1,0:T(8,128)(2,1)} %k_in.1, bf16[512,512]{1,0:T(8,128)(2,1)} %v_in.1, s32[4,20]{1,0:T(4,128)} %level_in.1, bf16[512,2048]{1,0:T(8,128)(2,1)} %grad_in.1), custom_call_target="tpu_custom_call" | custom-call | tf_op jit(solution)/shard_map/pallas_call | solution.py:605
  66.4 0.8 %copy.9 = bf16[512,512]{1,0:T(8,128)(2,1)} copy(bf16[512,512]{1,0:T(8,128)(2,1)S(1)} %get-tuple-element.2) | data formatting | bytes 1048576
  67.2 0.8 %copy.10 = f32[256,512]{1,0:T(8,128)} copy(f32[256,512]{1,0:T(8,128)S(1)} %get-tuple-element.3) | data formatting | bytes 1048576
